TPU v7x, 256 devices: a whole 4x4x8 slice. The times are simulated.
256 devices in a mesh: contact: 32 (over y, x, core), body: 8 (over z).
Axes of the slice: x: 4, y: 4, z: 8, core: 2. Of those that a mesh axis runs over, the one named last changes fastest.
Arguments:
- jacobian: bfloat16 [4096, 2, 384, 384], P(('contact', 'body')), may hold values from -0.21875 to 0.21875
- tile_block: int32 [4096, 2], P(('contact', 'body')), may hold values from 0 to 31
- tile_count: int32 [256], P(('contact', 'body')), may hold values from 8 to 16, as said below
- vel_free: float32 [256, 384], P('body'), may hold values from -6 to 6
- inv_mass: float32 [256, 384], P('body'), may hold values from 0.25 to 2
- bias: float32 [4096, 384], P(('contact', 'body')), may hold values from -6 to 6
- step_scale: float32 [4096, 384], P(('contact', 'body')), may hold values from 0.05 to 0.5
- friction: float32 [4096, 128], P(('contact', 'body')), may hold values from 0.2 to 1
- impulse_start: float32 [4096, 384], P(('contact', 'body')), may hold values from -6 to 6
Outputs:
- impulse: float32 [4096, 384], P(('contact', 'body'))
- velocity: float32 [256, 384], P('body')
Inputs may be any that keep to these rules, and one draw needn't show every extreme that they name: `tile_count`: some device has all 16 tile slots live in every draw.
All inputs are finite; a program needn't handle non-finite values.
Results may differ from a plain program's by a relative error of at most 0.0062.
Values may be sent and summed in bfloat16 or wider, within the bound.
A program may use at most 64 MiB of HBM per device.

v0:
```python
import jax
import jax.numpy as jnp
from jax import lax
from jax.sharding import PartitionSpec as P

ITERS = 2


def shifted(value, axis, steps):
    count = lax.axis_size(axis)
    pairs = [(source, (source + steps) % count) for source in range(count)]
    return lax.ppermute(value, axis, pairs)


def project(trial, friction, contacts):
    normal = trial[:, :contacts]
    first = trial[:, contacts : 2 * contacts]
    second = trial[:, 2 * contacts :]
    tangent = jnp.sqrt(first * first + second * second)
    inside = tangent <= friction * normal
    below = friction * tangent <= -normal
    moved = (normal + friction * tangent) / (1.0 + friction * friction)
    safe = jnp.where(inside | below, 1.0, tangent)
    factor = jnp.where(inside, 1.0, jnp.where(below, 0.0, friction * moved / safe))
    new_normal = jnp.where(inside, normal, jnp.where(below, 0.0, moved))
    return jnp.concatenate([new_normal, first * factor, second * factor], axis=1)


def per_device(
    jacobian, tile_block, tile_count, vel_free, inv_mass, bias, step_scale, friction, impulse_start
):
    tiles_here = jacobian.shape[0]
    slab_blocks = vel_free.shape[0]
    contacts = friction.shape[1]
    order = jnp.arange(tiles_here, dtype=jnp.int32)
    mask = (order < tile_count[0]).astype(jnp.float32)[:, None]
    span = jnp.arange(slab_blocks, dtype=jnp.int32)
    pick_own = (tile_block[:, 0:1] == span[None, :]).astype(jnp.float32)
    pick_next = (tile_block[:, 1:2] == span[None, :]).astype(jnp.float32)
    pick_own_b = pick_own.astype(jnp.bfloat16)
    pick_next_b = pick_next.astype(jnp.bfloat16)

    def merged_partials(lam):
        lamb = lam.astype(jnp.bfloat16)
        push = jnp.einsum("tkbc,tc->tkb", jacobian, lamb, preferred_element_type=jnp.float32)
        own = jnp.einsum("ts,tb->sb", pick_own, push[:, 0], precision=lax.Precision.HIGHEST)
        later = jnp.einsum("ts,tb->sb", pick_next, push[:, 1], precision=lax.Precision.HIGHEST)
        return own + shifted(later, "body", 1)

    def slab_total(lam):
        return lax.psum(merged_partials(lam), "contact")

    lam = impulse_start * mask
    for sweep in range(ITERS):
        total = slab_total(lam)
        velb = (vel_free + inv_mass * total).astype(jnp.bfloat16)
        velb_next = shifted(velb, "body", -1)
        rows_own = jnp.dot(pick_own_b, velb, preferred_element_type=jnp.float32).astype(
            jnp.bfloat16
        )
        rows_next = jnp.dot(pick_next_b, velb_next, preferred_element_type=jnp.float32).astype(
            jnp.bfloat16
        )
        rows = jnp.stack([rows_own, rows_next], axis=1)
        rel = jnp.einsum("tkbc,tkb->tc", jacobian, rows, preferred_element_type=jnp.float32) + bias
        lam = project(lam - step_scale * rel, friction, contacts) * mask
    total = slab_total(lam)
    velocity = vel_free + inv_mass * total
    return (lam, velocity)


def solution(mesh):
    placed = (
        P(("contact", "body"), None, None, None),
        P(("contact", "body"), None),
        P(("contact", "body")),
        P("body", None),
        P("body", None),
        P(("contact", "body"), None),
        P(("contact", "body"), None),
        P(("contact", "body"), None),
        P(("contact", "body"), None),
    )
    return jax.shard_map(
        per_device,
        mesh=mesh,
        in_specs=placed,
        out_specs=(P(("contact", "body"), None), P("body", None)),
        check_vma=False,
    )
```

profile of v0, /device:TPU:0, one launch (start us, length us, event | category | flops | bytes accessed | tf_op | source)
XLA Modules:
  0.0 435.7 jit_solution(17397203647870327549)
XLA Ops:
  0.6 0.0 copy-start.1
  0.6 0.0 copy-start
  1.3 0.8 slice_bitcast_fusion.1
  2.1 0.8 fusion.35
  2.9 0.0 copy-start.2
  2.9 0.0 copy-start.3
  2.9 0.0 copy-start.4
  2.9 0.0 copy-start.5
  2.9 6.2 %fusion.31 = f32[16,1,2,384]{3,1,2,0:T(1,128)S(1)} fusion(bf16[16,2,384,384]{3,2,1,0:T(8,128)(2,1)} %param.9, bf16[16,384,1,1]{1,0,2,3:T(8,128)(2,1)S(1)} %fusion.35), kind=kOutput, calls=%fused_computation.50 | convolution fusion | flops 9437184 | bytes 9498624 | tf_op jit(solution)/shard_map/tkbc,tc->tkb/dot_general | solution.py:45
  9.3 0.3 fusion.18
  9.6 0.3 collective-permute-start
  9.8 6.0 %collective-permute-done = f32[32,384]{1,0:T(8,128)S(1)} collective-permute-done((f32[32,384]{1,0:T(8,128)S(1)}, f32[32,384]{1,0:T(8,128)S(1)}, u32[]{:S(2)}, u32[]{:S(2)}) %collective-permute-start) | collective-permute-done | bytes 49184 | tf_op jit(solution)/shard_map/ppermute | solution.py:12
  15.8 0.3 convolution_add_fusion.2
  16.1 127.5 %psum.21 = f32[32,384]{1,0:T(8,128)S(1)} all-reduce(f32[32,384]{1,0:T(8,128)S(1)} %convolution_add_fusion.2), channel_id=1, replica_groups=mesh['contact'=32,'body'=8] {'contact'}, use_global_device_ids=true, to_apply=%region_0.0 | all-reduce | flops 12288 | bytes 98304 | tf_op jit(solution)/shard_map/psum | solution.py:51
  143.6 0.0 copy-done.1
  143.6 0.0 copy-done
  143.7 1.8 collective-permute-start.1
  145.5 0.2 fusion
  145.7 1.9 collective-permute-done.1
  147.6 0.2 fusion.1
  147.8 5.0 %fusion.6 = f32[16,1,384,1]{2,1,3,0:T(1,128)S(1)} fusion(bf16[16,2,384,384]{3,2,1,0:T(8,128)(2,1)} %param.9, bf16[16,2,384,1]{2,0,1,3:T(8,128)(2,1)S(1)} %maximum_bitcast_fusion), kind=kOutput, calls=%fused_computation.15 | convolution fusion | flops 9437184 | bytes 9486336 | tf_op jit(solution)/shard_map/tkbc,tkb->tc/dot_general | solution.py:65
  152.8 0.0 copy-done.2
  152.8 0.0 copy-done.3
  152.8 0.0 copy-done.4
  152.8 0.1 fusion.26
  152.9 0.0 copy-done.5
  152.9 0.1 fusion.34
  153.0 6.2 %fusion.29 = f32[16,1,2,384]{3,1,2,0:T(1,128)S(1)} fusion(bf16[16,2,384,384]{3,2,1,0:T(8,128)(2,1)} %param.9, bf16[16,384,1,1]{1,0,2,3:T(8,128)(2,1)S(1)} %fusion.34), kind=kOutput, calls=%fused_computation.48 | convolution fusion | flops 9437184 | bytes 9498624 | tf_op jit(solution)/shard_map/tkbc,tc->tkb/dot_general | solution.py:45
  159.3 0.3 fusion.13
  159.6 0.1 collective-permute-start.2
  159.7 5.3 %collective-permute-done.2 = f32[32,384]{1,0:T(8,128)S(1)} collective-permute-done((f32[32,384]{1,0:T(8,128)S(1)}, f32[32,384]{1,0:T(8,128)S(1)}, u32[]{:S(2)}, u32[]{:S(2)}) %collective-permute-start.2) | collective-permute-done | bytes 49184 | tf_op jit(solution)/shard_map/ppermute | solution.py:12
  165.0 0.3 convolution_add_fusion.1
  165.3 123.8 %psum.22 = f32[32,384]{1,0:T(8,128)S(1)} all-reduce(f32[32,384]{1,0:T(8,128)S(1)} %convolution_add_fusion.1), channel_id=1, replica_groups=mesh['contact'=32,'body'=8] {'contact'}, use_global_device_ids=true, to_apply=%region_1.2 | all-reduce | flops 12288 | bytes 98304 | tf_op jit(solution)/shard_map/psum | solution.py:51
  289.1 1.8 collective-permute-start.3
  290.9 0.2 fusion.2
  291.1 1.9 collective-permute-done.3
  293.0 0.2 fusion.3
  293.2 5.0 %fusion.4 = f32[16,1,384,1]{2,1,3,0:T(1,128)S(1)} fusion(bf16[16,2,384,384]{3,2,1,0:T(8,128)(2,1)} %param.9, bf16[16,2,384,1]{2,0,1,3:T(8,128)(2,1)S(1)} %maximum_bitcast_fusion.1), kind=kOutput, calls=%fused_computation.12 | convolution fusion | flops 9437184 | bytes 9486336 | tf_op jit(solution)/shard_map/tkbc,tkb->tc/dot_general | solution.py:65
  298.2 0.1 fusion.24
  298.4 0.7 convert_bitcast_fusion
  299.1 6.2 %fusion.27 = f32[16,1,2,384]{3,1,2,0:T(1,128)S(1)} fusion(bf16[16,2,384,384]{3,2,1,0:T(8,128)(2,1)} %param.9, bf16[16,384,1,1]{1,0,2,3:T(8,128)(2,1)S(1)} %get-tuple-element.2), kind=kOutput, calls=%fused_computation.46 | convolution fusion | flops 9437184 | bytes 9498624 | tf_op jit(solution)/shard_map/tkbc,tc->tkb/dot_general | solution.py:45
  305.4 0.3 fusion.8
  305.6 0.1 collective-permute-start.4
  305.7 5.3 %collective-permute-done.4 = f32[32,384]{1,0:T(8,128)S(1)} collective-permute-done((f32[32,384]{1,0:T(8,128)S(1)}, f32[32,384]{1,0:T(8,128)S(1)}, u32[]{:S(2)}, u32[]{:S(2)}) %collective-permute-start.4) | collective-permute-done | bytes 49184 | tf_op jit(solution)/shard_map/ppermute | solution.py:12
  311.0 0.3 convolution_add_fusion
  311.3 123.8 %psum.23 = f32[32,384]{1,0:T(8,128)S(1)} all-reduce(f32[32,384]{1,0:T(8,128)S(1)} %convolution_add_fusion), channel_id=1, replica_groups=mesh['contact'=32,'body'=8] {'contact'}, use_global_device_ids=true, to_apply=%region_2.3 | all-reduce | flops 12288 | bytes 98304 | tf_op jit(solution)/shard_map/psum | solution.py:51
  435.1 0.6 multiply_add_fusion
  (15 shorter events, 0.3 us)
Async XLA Ops:
  0.6 143.0 %copy-start.1 = (f32[32,384]{1,0:T(8,128)S(1)}, f32[32,384]{1,0:T(8,128)}, u32[]{:S(2)}) copy-start(f32[32,384]{1,0:T(8,128)} %param.13) | copy-start | bytes 147460
  0.6 143.0 %copy-start = (f32[32,384]{1,0:T(8,128)S(1)}, f32[32,384]{1,0:T(8,128)}, u32[]{:S(2)}) copy-start(f32[32,384]{1,0:T(8,128)} %param.12) | copy-start | bytes 147460
  2.9 149.9 %copy-start.2 = (f32[16,384]{1,0:T(8,128)S(1)}, f32[16,384]{1,0:T(8,128)}, u32[]{:S(2)}) copy-start(f32[16,384]{1,0:T(8,128)} %param.17) | copy-start | bytes 73732
  2.9 149.9 %copy-start.3 = (f32[16,384]{1,0:T(8,128)S(1)}, f32[16,384]{1,0:T(8,128)}, u32[]{:S(2)}) copy-start(f32[16,384]{1,0:T(8,128)} %param.15) | copy-start | bytes 73732
  2.9 149.9 %copy-start.4 = (f32[16,384]{1,0:T(8,128)S(1)}, f32[16,384]{1,0:T(8,128)}, u32[]{:S(2)}) copy-start(f32[16,384]{1,0:T(8,128)} %param.14) | copy-start | bytes 73732
  2.9 150.0 %copy-start.5 = (f32[16,128]{1,0:T(8,128)S(1)}, f32[16,128]{1,0:T(8,128)}, u32[]{:S(2)}) copy-start(f32[16,128]{1,0:T(8,128)} %param.16) | copy-start | bytes 24580
  9.6 6.3 %collective-permute-start = (f32[32,384]{1,0:T(8,128)S(1)}, f32[32,384]{1,0:T(8,128)S(1)}, u32[]{:S(2)}, u32[]{:S(2)}) collective-permute-start(f32[32,384]{1,0:T(8,128)S(1)} %fusion.18), channel_id=1, source_target_pairs={{0,1},{1,2},{2,3},{3,4},{4,5},{5,6},{6,7},{7,0},{8,9},{9,10},{10,1... | collective-permute-start | bytes 147464 | tf_op jit(solution)/shard_map/ppermute | solution.py:12
  143.7 3.9 collective-permute-start.1
  159.6 5.4 %collective-permute-start.2 = (f32[32,384]{1,0:T(8,128)S(1)}, f32[32,384]{1,0:T(8,128)S(1)}, u32[]{:S(2)}, u32[]{:S(2)}) collective-permute-start(f32[32,384]{1,0:T(8,128)S(1)} %fusion.13), channel_id=1, source_target_pairs={{0,1},{1,2},{2,3},{3,4},{4,5},{5,6},{6,7},{7,0},{8,9},{9,10},{10,1... | collective-permute-start | bytes 147464 | tf_op jit(solution)/shard_map/ppermute | solution.py:12
  289.1 3.9 collective-permute-start.3
  305.6 5.4 %collective-permute-start.4 = (f32[32,384]{1,0:T(8,128)S(1)}, f32[32,384]{1,0:T(8,128)S(1)}, u32[]{:S(2)}, u32[]{:S(2)}) collective-permute-start(f32[32,384]{1,0:T(8,128)S(1)} %fusion.8), channel_id=1, source_target_pairs={{0,1},{1,2},{2,3},{3,4},{4,5},{5,6},{6,7},{7,0},{8,9},{9,10},{10,1... | collective-permute-start | bytes 147464 | tf_op jit(solution)/shard_map/ppermute | solution.py:12
where the time goes:
time: 436 us
  blocking collectives  375 us (86%)
  matrix products  31.2 us (7%)
  waiting for transfers between devices  20.4 us (5%)
    psum x3, blocking collectives, slab_total(): return lax.psum(merged_partials(lam), 'contact')  375 us
    ppermute x5, waiting for transfers between devices, shifted(): return lax.ppermute(value, axis, pairs)  20.4 us
    dot_general x3, matrix products, merged_partials(): jnp.einsum('tkbc,tc->tkb', jacobian, lamb, preferred_element_type=jnp.flo...  18.7 us
    dot_general x2, matrix products, per_device(): jnp.einsum('tkbc,tkb->tc', jacobian, rows, preferred_element_type=jnp.flo...  10.1 us
  transfers between devices with their start and end apart: 5, of which 5 were waited for; matrix products, arithmetic and copies ran while one was open for 0% of the time, Pallas kernels for 0%

commit v1 on v0

--- a/solution.py
+++ b/solution.py
@@ -48,7 +48,7 @@
         return own + shifted(later, "body", 1)
 
     def slab_total(lam):
-        return lax.psum(merged_partials(lam), "contact")
+        return jnp.sum(lax.all_gather(merged_partials(lam), "contact"), axis=0)
 
     lam = impulse_start * mask
     for sweep in range(ITERS):

time: 436 us -> 228 us (0.52)
  blocking collectives: 375 us -> 0 us
  waiting for transfers between devices: 20.4 us -> 160 us
  between operations: 1.5 us -> 14.6 us
  other arithmetic: 2.45 us -> 6.94 us
  starting transfers between devices: 4.05 us -> 8.41 us
    psum x3 -> x0, blocking collectives: 375 us -> none  [slab_total(): return lax.psum(merged_partials(lam), 'contact')]
    all_gather x0 -> x3, waiting for transfers between devices: none -> 142 us  [slab_total(): return jnp.sum(lax.all_gather(merged_partials(lam), 'contact'), axis=0)]
    reduce_sum x0 -> x3, other arithmetic: none -> 4.49 us  [slab_total(): return jnp.sum(lax.all_gather(merged_partials(lam), 'contact'), axis=0)]
  transfers between devices with their start and end apart: 5 -> 8, of which waited for: 5 -> 8; matrix products, arithmetic and copies ran while one was open for 0% -> 0% of each run, Pallas kernels for 0% -> 0%
where the time goes in v1:
time: 228 us; the launch traced here: 225 us
  waiting for transfers between devices  160 us (70%)
  matrix products  33.1 us (15%)
  between operations  14.6 us (6%)
  starting transfers between devices  8.41 us (4%)
  other arithmetic  6.94 us (3%)
    all_gather x3, waiting for transfers between devices, slab_total(): return jnp.sum(lax.all_gather(merged_partials(lam), 'contact'), axis=0)  142 us
    ppermute x5, waiting for transfers between devices, shifted(): return lax.ppermute(value, axis, pairs)  18.7 us
    dot_general x3, matrix products, merged_partials(): jnp.einsum('tkbc,tc->tkb', jacobian, lamb, preferred_element_type=jnp.flo...  18.7 us
    dot_general x2, matrix products, per_device(): jnp.einsum('tkbc,tkb->tc', jacobian, rows, preferred_element_type=jnp.flo...  10.1 us
    ppermute x5, starting transfers between devices, shifted(): return lax.ppermute(value, axis, pairs)  8.29 us
  transfers between devices with their start and end apart: 8, of which 8 were waited for; matrix products, arithmetic and copies ran while one was open for 0% of the time, Pallas kernels for 0%

profile of v1, /device:TPU:0, one launch (start us, length us, event | category | flops | bytes accessed | tf_op | source)
XLA Modules:
  0.0 224.5 jit_solution(5508725166102968278)
XLA Ops:
  7.2 0.0 copy-start.1
  7.2 0.0 copy-start
  7.2 0.0 all-gather.7.cloned.1.call-start
  7.9 0.8 slice_bitcast_fusion.1
  8.6 0.8 fusion.35
  9.5 0.0 copy-start.5
  9.5 6.2 %fusion.31 = f32[16,1,2,384]{3,1,2,0:T(1,128)S(1)} fusion(bf16[16,2,384,384]{3,2,1,0:T(8,128)(2,1)} %param.9, bf16[16,384,1,1]{1,0,2,3:T(8,128)(2,1)S(1)} %fusion.35), kind=kOutput, calls=%fused_computation.50 | convolution fusion | flops 9437184 | bytes 9498624 | tf_op jit(solution)/shard_map/tkbc,tc->tkb/dot_general | solution.py:45
  15.8 0.3 fusion.18
  16.1 0.3 collective-permute-start
  16.4 6.0 %collective-permute-done = f32[32,384]{1,0:T(8,128)S(1)} collective-permute-done((f32[32,384]{1,0:T(8,128)S(1)}, f32[32,384]{1,0:T(8,128)S(1)}, u32[]{:S(2)}, u32[]{:S(2)}) %collective-permute-start) | collective-permute-done | bytes 49184 | tf_op jit(solution)/shard_map/ppermute | solution.py:12
  22.4 0.9 convolution_add_fusion.2
  23.3 0.0 all-gather.7.cloned.1.call-update
  23.3 0.0 all-gather.9.cloned.1.call-start
  23.4 48.7 %all-gather.7.cloned.1.call-done = f32[1024,384]{1,0:T(8,128)} async-done(((f32[32,384]{1,0:T(8,128)}), f32[1024,384]{1,0:T(8,128)}) %all-gather.7.cloned.1.call-update) | async-done | bytes 1572880 | tf_op jit(solution)/shard_map/all_gather | solution.py:51
  72.1 1.5 reduce_sum.27
  73.6 3.4 %collective-permute-start.1 = (bf16[32,384]{1,0:T(8,128)(2,1)S(1)}, bf16[32,384]{1,0:T(8,128)(2,1)S(1)}, u32[]{:S(2)}, u32[]{:S(2)}) collective-permute-start(bf16[32,384]{1,0:T(8,128)(2,1)S(1)} %add_convert_fusion.1), channel_id=1, source_target_pairs={{0,7},{1,0},{2,1},{3,2},{4,3},{5,4},{6,5},{7,6},{8,15},{9,8},{10,9... | collective-permute-start | bytes 73736 | tf_op jit(solution)/shard_map/ppermute | solution.py:12
  77.0 0.2 fusion
  77.2 1.3 collective-permute-done.1
  78.5 0.2 fusion.1
  78.7 5.0 %fusion.6 = f32[16,1,384,1]{2,1,3,0:T(1,128)S(1)} fusion(bf16[16,2,384,384]{3,2,1,0:T(8,128)(2,1)} %param.9, bf16[16,2,384,1]{2,0,1,3:T(8,128)(2,1)S(1)} %maximum_bitcast_fusion), kind=kOutput, calls=%fused_computation.15 | convolution fusion | flops 9437184 | bytes 9486336 | tf_op jit(solution)/shard_map/tkbc,tkb->tc/dot_general | solution.py:65
  83.8 0.0 copy-done.4
  83.8 0.1 fusion.26
  83.9 0.1 fusion.34
  84.0 6.2 %fusion.29 = f32[16,1,2,384]{3,1,2,0:T(1,128)S(1)} fusion(bf16[16,2,384,384]{3,2,1,0:T(8,128)(2,1)} %param.9, bf16[16,384,1,1]{1,0,2,3:T(8,128)(2,1)S(1)} %fusion.34), kind=kOutput, calls=%fused_computation.48 | convolution fusion | flops 9437184 | bytes 9498624 | tf_op jit(solution)/shard_map/tkbc,tc->tkb/dot_general | solution.py:45
  90.3 0.3 fusion.13
  90.6 0.6 collective-permute-start.2
  91.2 5.0 %collective-permute-done.2 = f32[32,384]{1,0:T(8,128)S(1)} collective-permute-done((f32[32,384]{1,0:T(8,128)S(1)}, f32[32,384]{1,0:T(8,128)S(1)}, u32[]{:S(2)}, u32[]{:S(2)}) %collective-permute-start.2) | collective-permute-done | bytes 49184 | tf_op jit(solution)/shard_map/ppermute | solution.py:12
  96.2 0.9 convolution_add_fusion.1
  97.1 0.0 all-gather.9.cloned.1.call-update
  97.2 0.0 all-gather.11.cloned.1.call-start
  97.2 46.5 %all-gather.9.cloned.1.call-done = f32[1024,384]{1,0:T(8,128)} async-done(((f32[32,384]{1,0:T(8,128)}), f32[1024,384]{1,0:T(8,128)}) %all-gather.9.cloned.1.call-update) | async-done | bytes 1572880 | tf_op jit(solution)/shard_map/all_gather | solution.py:51
  143.7 1.5 reduce_sum.28
  145.2 3.4 %collective-permute-start.3 = (bf16[32,384]{1,0:T(8,128)(2,1)S(1)}, bf16[32,384]{1,0:T(8,128)(2,1)S(1)}, u32[]{:S(2)}, u32[]{:S(2)}) collective-permute-start(bf16[32,384]{1,0:T(8,128)(2,1)S(1)} %add_convert_fusion), channel_id=1, source_target_pairs={{0,7},{1,0},{2,1},{3,2},{4,3},{5,4},{6,5},{7,6},{8,15},{9,8},{10,9... | collective-permute-start | bytes 73736 | tf_op jit(solution)/shard_map/ppermute | solution.py:12
  148.6 0.2 fusion.2
  148.8 1.3 collective-permute-done.3
  150.1 0.2 fusion.3
  150.3 5.0 %fusion.4 = f32[16,1,384,1]{2,1,3,0:T(1,128)S(1)} fusion(bf16[16,2,384,384]{3,2,1,0:T(8,128)(2,1)} %param.9, bf16[16,2,384,1]{2,0,1,3:T(8,128)(2,1)S(1)} %maximum_bitcast_fusion.1), kind=kOutput, calls=%fused_computation.12 | convolution fusion | flops 9437184 | bytes 9486336 | tf_op jit(solution)/shard_map/tkbc,tkb->tc/dot_general | solution.py:65
  155.4 0.1 fusion.24
  155.5 0.7 convert_bitcast_fusion
  156.2 6.2 %fusion.27 = f32[16,1,2,384]{3,1,2,0:T(1,128)S(1)} fusion(bf16[16,2,384,384]{3,2,1,0:T(8,128)(2,1)} %param.9, bf16[16,384,1,1]{1,0,2,3:T(8,128)(2,1)S(1)} %get-tuple-element.2), kind=kOutput, calls=%fused_computation.46 | convolution fusion | flops 9437184 | bytes 9498624 | tf_op jit(solution)/shard_map/tkbc,tc->tkb/dot_general | solution.py:45
  162.5 0.3 fusion.8
  162.8 0.6 collective-permute-start.4
  163.4 5.0 %collective-permute-done.4 = f32[32,384]{1,0:T(8,128)S(1)} collective-permute-done((f32[32,384]{1,0:T(8,128)S(1)}, f32[32,384]{1,0:T(8,128)S(1)}, u32[]{:S(2)}, u32[]{:S(2)}) %collective-permute-start.4) | collective-permute-done | bytes 49184 | tf_op jit(solution)/shard_map/ppermute | solution.py:12
  168.4 0.9 convolution_add_fusion
  169.3 0.0 all-gather.11.cloned.1.call-update
  169.3 46.5 %all-gather.11.cloned.1.call-done = f32[1024,384]{1,0:T(8,128)} async-done(((f32[32,384]{1,0:T(8,128)}), f32[1024,384]{1,0:T(8,128)}) %all-gather.11.cloned.1.call-update) | async-done | bytes 1572880 | tf_op jit(solution)/shard_map/all_gather | solution.py:51
  215.9 1.5 reduce_sum.29
  217.4 0.6 multiply_add_fusion
  (23 shorter events, 0.4 us)
Async XLA Ops:
  7.2 66.4 %copy-start.1 = (f32[32,384]{1,0:T(8,128)S(1)}, f32[32,384]{1,0:T(8,128)}, u32[]{:S(2)}) copy-start(f32[32,384]{1,0:T(8,128)} %param.13) | copy-start | bytes 147460
  7.2 66.4 %copy-start = (f32[32,384]{1,0:T(8,128)S(1)}, f32[32,384]{1,0:T(8,128)}, u32[]{:S(2)}) copy-start(f32[32,384]{1,0:T(8,128)} %param.12) | copy-start | bytes 147460
  7.2 64.9 %all-gather.7.cloned.1.call-start = ((), (), s32[]{:S(2)}) async-start(), calls=%async_computation | async-start | bytes 1622016 | tf_op jit(solution)/shard_map/all_gather | solution.py:51
  9.5 74.3 %copy-start.2 = (f32[16,384]{1,0:T(8,128)S(1)}, f32[16,384]{1,0:T(8,128)}, u32[]{:S(2)}) copy-start(f32[16,384]{1,0:T(8,128)} %param.17) | copy-start | bytes 73732
  9.5 74.3 %copy-start.3 = (f32[16,384]{1,0:T(8,128)S(1)}, f32[16,384]{1,0:T(8,128)}, u32[]{:S(2)}) copy-start(f32[16,384]{1,0:T(8,128)} %param.15) | copy-start | bytes 73732
  9.5 74.3 %copy-start.4 = (f32[16,384]{1,0:T(8,128)S(1)}, f32[16,384]{1,0:T(8,128)}, u32[]{:S(2)}) copy-start(f32[16,384]{1,0:T(8,128)} %param.14) | copy-start | bytes 73732
  9.5 74.4 %copy-start.5 = (f32[16,128]{1,0:T(8,128)S(1)}, f32[16,128]{1,0:T(8,128)}, u32[]{:S(2)}) copy-start(f32[16,128]{1,0:T(8,128)} %param.16) | copy-start | bytes 24580
  16.1 6.3 %collective-permute-start = (f32[32,384]{1,0:T(8,128)S(1)}, f32[32,384]{1,0:T(8,128)S(1)}, u32[]{:S(2)}, u32[]{:S(2)}) collective-permute-start(f32[32,384]{1,0:T(8,128)S(1)} %fusion.18), channel_id=1, source_target_pairs={{0,1},{1,2},{2,3},{3,4},{4,5},{5,6},{6,7},{7,0},{8,9},{9,10},{10,1... | collective-permute-start | bytes 147464 | tf_op jit(solution)/shard_map/ppermute | solution.py:12
  23.3 120.4 %all-gather.9.cloned.1.call-start = ((), (), s32[]{:S(2)}) async-start(), calls=%async_computation.1 | async-start | bytes 1622016 | tf_op jit(solution)/shard_map/all_gather | solution.py:51
  73.6 4.9 %collective-permute-start.1 = (bf16[32,384]{1,0:T(8,128)(2,1)S(1)}, bf16[32,384]{1,0:T(8,128)(2,1)S(1)}, u32[]{:S(2)}, u32[]{:S(2)}) collective-permute-start(bf16[32,384]{1,0:T(8,128)(2,1)S(1)} %add_convert_fusion.1), channel_id=1, source_target_pairs={{0,7},{1,0},{2,1},{3,2},{4,3},{5,4},{6,5},{7,6},{8,15},{9,8},{10,9... | collective-permute-start | bytes 73736 | tf_op jit(solution)/shard_map/ppermute | solution.py:12
  90.6 5.7 %collective-permute-start.2 = (f32[32,384]{1,0:T(8,128)S(1)}, f32[32,384]{1,0:T(8,128)S(1)}, u32[]{:S(2)}, u32[]{:S(2)}) collective-permute-start(f32[32,384]{1,0:T(8,128)S(1)} %fusion.13), channel_id=1, source_target_pairs={{0,1},{1,2},{2,3},{3,4},{4,5},{5,6},{6,7},{7,0},{8,9},{9,10},{10,1... | collective-permute-start | bytes 147464 | tf_op jit(solution)/shard_map/ppermute | solution.py:12
  97.2 118.7 %all-gather.11.cloned.1.call-start = ((), (), s32[]{:S(2)}) async-start(), calls=%async_computation.2 | async-start | bytes 1622016 | tf_op jit(solution)/shard_map/all_gather | solution.py:51
  145.2 4.9 %collective-permute-start.3 = (bf16[32,384]{1,0:T(8,128)(2,1)S(1)}, bf16[32,384]{1,0:T(8,128)(2,1)S(1)}, u32[]{:S(2)}, u32[]{:S(2)}) collective-permute-start(bf16[32,384]{1,0:T(8,128)(2,1)S(1)} %add_convert_fusion), channel_id=1, source_target_pairs={{0,7},{1,0},{2,1},{3,2},{4,3},{5,4},{6,5},{7,6},{8,15},{9,8},{10,9... | collective-permute-start | bytes 73736 | tf_op jit(solution)/shard_map/ppermute | solution.py:12
  162.8 5.7 %collective-permute-start.4 = (f32[32,384]{1,0:T(8,128)S(1)}, f32[32,384]{1,0:T(8,128)S(1)}, u32[]{:S(2)}, u32[]{:S(2)}) collective-permute-start(f32[32,384]{1,0:T(8,128)S(1)} %fusion.8), channel_id=1, source_target_pairs={{0,1},{1,2},{2,3},{3,4},{4,5},{5,6},{6,7},{7,0},{8,9},{9,10},{10,1... | collective-permute-start | bytes 147464 | tf_op jit(solution)/shard_map/ppermute | solution.py:12
Sparse Core Ops, SparseCore 0:
  23.4 48.5 all-gather.6
  97.3 46.3 all-gather.8
  169.5 46.3 all-gather.10
